TPU v7x, 32 devices: a whole 2x2x4 slice. The times are simulated.
32 devices in a mesh: dp: 8 (over z, y), seq: 4 (over x, core).
Axes of the slice: x: 2, y: 2, z: 4, core: 2. Of those that a mesh axis runs over, the one named last changes fastest.
Arguments:
- hidden_states: bfloat16 [4096, 2048], P(('dp', 'seq'))
- query_weight: bfloat16 [2048, 512], P('dp')
- key_weight: bfloat16 [2048, 128], P('dp')
- value_weight: bfloat16 [2048, 128], P('dp'), may hold values from -0.125 to 0.125
- doc_lengths: int32 [8, 8], P('dp'), may hold values from 1 to 256, 512 in all within a row
Outputs:
- context: bfloat16 [4096, 512], P(('dp', 'seq'))
Inputs may be any that keep to these rules, and one draw needn't show every extreme that they name: `doc_lengths`: each row sums to 512, and its longest document has exactly 256 tokens.
All inputs are finite; a program needn't handle non-finite values.
Results may differ from a plain program's by a relative error of at most 0.0076.
Values may be sent and summed in bfloat16 or wider, within the bound.
A program may use at most 64 MiB of HBM per device.

v0:
```python
import math
import jax
import jax.numpy as jnp
from jax import lax
from jax.sharding import PartitionSpec as P

HD = 64
EPSILON = 1e-05
THETA = 500000.0
NEG_FILL = -1e30


def normalize(states):
    floats = states.astype(jnp.float32)
    scale = lax.rsqrt(jnp.mean(floats * floats, axis=-1, keepdims=True) + EPSILON)
    return (floats * scale).astype(jnp.bfloat16)


def doc_offsets(doc_sizes, positions):
    ends = jnp.cumsum(doc_sizes)
    before = (ends[None, :] <= positions[:, None]).astype(jnp.int32)
    docs = jnp.sum(before, axis=1)
    starts = jnp.sum(before * doc_sizes[None, :], axis=1)
    return (docs, positions - starts)


def rotate(vectors, offset):
    half_dim = vectors.shape[-1] // 2
    index = jnp.arange(half_dim, dtype=jnp.float32)
    freqs = jnp.exp(index * (-2.0 / vectors.shape[-1]) * math.log(THETA))
    angle = offset.astype(jnp.float32)[:, None] * freqs[None, :]
    cosine = jnp.cos(angle)[:, None, :]
    sine = jnp.sin(angle)[:, None, :]
    first = vectors[..., :half_dim]
    second = vectors[..., half_dim:]
    return jnp.concatenate(
        [first * cosine - second * sine, second * cosine + first * sine], axis=-1
    )


def attend(queries, keys, values, docs):
    seq_length = queries.shape[0]
    group = queries.shape[1]
    scale = queries.shape[-1] ** (-0.5)
    block = math.gcd(256, seq_length)
    key_pos = jnp.arange(seq_length, dtype=jnp.int32)

    def one_block(number):
        first_row = number * block
        query_block = lax.dynamic_slice_in_dim(queries, first_row, block, 0)
        query_docs = lax.dynamic_slice_in_dim(docs, first_row, block, 0)
        query_pos = first_row + jnp.arange(block, dtype=jnp.int32)
        scores = (
            jnp.einsum("qgd,kd->gqk", query_block, keys, preferred_element_type=jnp.float32) * scale
        )
        allowed = (key_pos[None, :] <= query_pos[:, None]) & (docs[None, :] == query_docs[:, None])
        scores = jnp.where(allowed[None], scores, NEG_FILL)
        highest = jnp.max(scores, axis=-1, keepdims=True)
        expons = jnp.exp(scores - highest)
        totals = jnp.sum(expons, axis=-1, keepdims=True)
        weights = (expons / totals).astype(jnp.bfloat16)
        mixed = jnp.einsum("gqk,kd->qgd", weights, values, preferred_element_type=jnp.float32)
        return mixed.astype(jnp.bfloat16)

    blocks = lax.map(one_block, jnp.arange(seq_length // block, dtype=jnp.int32))
    return blocks.reshape(seq_length, group * queries.shape[-1])


def shards(hidden_states, query_weight, key_weight, value_weight, doc_lengths):
    tok_count = hidden_states.shape[0]
    seq_count = lax.axis_size("seq")
    seq_index = lax.axis_index("seq")
    seq_length = tok_count * seq_count
    head_dim = HD
    heads_here = query_weight.shape[1] // (head_dim * seq_count)
    kv_heads = key_weight.shape[1] // head_dim
    normed = normalize(hidden_states)
    doc_sizes = doc_lengths[0]
    all_positions = jnp.arange(seq_length, dtype=jnp.int32)
    docs_all, offset_all = doc_offsets(doc_sizes, all_positions)
    pieces = (
        lax.all_gather(query_weight, "dp", axis=0, tiled=True),
        lax.all_gather(key_weight, "dp", axis=0, tiled=True),
        lax.all_gather(value_weight, "dp", axis=0, tiled=True),
    )
    query_lin, key_lin, value_lin = tuple(
        (jnp.dot(normed, piece, preferred_element_type=jnp.float32) for piece in pieces)
    )
    own_offset = lax.dynamic_slice_in_dim(offset_all, seq_index * tok_count, tok_count, 0)
    query_rot = (
        rotate(query_lin.reshape(tok_count, -1, head_dim), own_offset)
        .astype(jnp.bfloat16)
        .reshape(tok_count, -1)
    )
    key_rot = rotate(key_lin.reshape(tok_count, kv_heads, head_dim), own_offset).astype(
        jnp.bfloat16
    )
    value_cast = value_lin.astype(jnp.bfloat16).reshape(tok_count, kv_heads, head_dim)
    key_value = jnp.concatenate([key_rot, value_cast], axis=2)
    repeated = jnp.repeat(key_value, seq_count // kv_heads, axis=1).reshape(tok_count, -1)
    query_heads, kv_local = (
        lax.all_to_all(query_rot, "seq", split_axis=1, concat_axis=0, tiled=True),
        lax.all_to_all(repeated, "seq", split_axis=1, concat_axis=0, tiled=True),
    )
    key_local = kv_local[:, :head_dim]
    value_local = kv_local[:, head_dim:]
    mixed_heads = attend(
        query_heads.reshape(seq_length, heads_here, head_dim), key_local, value_local, docs_all
    )
    return lax.all_to_all(mixed_heads, "seq", split_axis=0, concat_axis=1, tiled=True)


def solution(mesh):
    placed = (P(("dp", "seq"), None), P("dp", None), P("dp", None), P("dp", None), P("dp", None))
    return jax.shard_map(
        shards, mesh=mesh, in_specs=placed, out_specs=P(("dp", "seq"), None), check_vma=False
    )
```

profile of v0, /device:TPU:0, one launch (start us, length us, event | category | flops | bytes accessed | tf_op | source)
XLA Modules:
  0.0 120.7 jit_solution(3050384695510439155)
XLA Ops:
  6.5 0.0 copy-start
  6.5 0.0 copy-start.1
  6.5 0.0 all-gather.2.cloned.1.call-start
  6.5 0.7 all-gather.2.cloned.1.call-update
  7.3 0.8 reduce-window.8
  8.1 0.7 select_reduce_fusion
  8.9 0.1 dynamic-slice_convert_fusion
  8.9 1.2 %fusion.23 = f32[128]{0:T(128)S(1)} fusion(bf16[128,2048]{1,0:T(8,128)(2,1)} %param.7), kind=kLoop, calls=%fused_computation.27 | loop fusion | flops 786304 | bytes 524800 | tf_op jit(solution)/shard_map/reduce_sum | solution.py:15
  10.2 0.1 multiply_cosine_fusion
  10.3 34.1 %all_gather.10 = bf16[2048,128]{1,0:T(8,128)(2,1)S(1)} all-gather(bf16[256,128]{1,0:T(8,128)(2,1)} %param.9), channel_id=1, replica_groups=mesh['dp'=8,'seq'=4] {'dp'}, dimensions={0}, use_global_device_ids=true | all-gather | bytes 589824 | tf_op jit(solution)/shard_map/all_gather | solution.py:83
  44.5 1.4 %fusion.26 = f32[128,128]{0,1:T(8,128)S(1)} fusion(bf16[2048,128]{1,0:T(8,128)(2,1)S(1)} %all_gather.10, bf16[128,2048]{1,0:T(8,128)(2,1)} %param.7, f32[128]{0:T(128)S(1)} %add_rsqrt_fusion), kind=kOutput, calls=%fused_computation.44 | convolution fusion | flops 67895296 | bytes 1114624 | tf_op jit(solution)/shard_map/dot_general | solution.py:87
  45.9 0.0 copy-done.1
  45.9 32.3 %all_gather.11 = bf16[2048,128]{1,0:T(8,128)(2,1)S(1)} all-gather(bf16[256,128]{1,0:T(8,128)(2,1)S(1)} %copy-done.1), channel_id=1, replica_groups=mesh['dp'=8,'seq'=4] {'dp'}, dimensions={0}, use_global_device_ids=true | all-gather | bytes 589824 | tf_op jit(solution)/shard_map/all_gather | solution.py:84
  78.2 0.0 copy-done
  78.2 0.4 convolution_convert_fusion.1
  78.7 0.7 broadcast_in_dim.16
  79.3 3.3 %all-to-all-start.1 = ((bf16[128,4,128]{0,2,1:T(8,128)(2,1)}), bf16[128,4,128]{0,2,1:T(8,128)(2,1)S(1)}, u32[]{:S(2)}, u32[]{:S(2)}) async-start(bf16[128,4,128]{0,2,1:T(8,128)(2,1)} %bitcast.8), calls=%async_computation.1 | async-start | bytes 262144 | tf_op jit(solution)/shard_map/all_to_all | solution.py:103
  82.7 4.6 %all-to-all-done.1 = bf16[128,4,128]{0,2,1:T(8,128)(2,1)S(1)} async-done(((bf16[128,4,128]{0,2,1:T(8,128)(2,1)}), bf16[128,4,128]{0,2,1:T(8,128)(2,1)S(1)}, u32[]{:S(2)}, u32[]{:S(2)}) %all-to-all-start.1) | async-done | bytes 131104 | tf_op jit(solution)/shard_map/all_to_all | solution.py:103
  87.2 0.1 copy.34
  87.4 0.0 all-gather.2.cloned.1.call-done
  87.4 2.6 %fusion.28 = f32[128,512]{0,1:T(8,128)S(1)} fusion(bf16[2048,512]{1,0:T(8,128)(2,1)} %all-gather.2.cloned.1.call-done, bf16[128,2048]{1,0:T(8,128)(2,1)S(1)} %copy-done, f32[128]{0:T(128)S(1)} %add_rsqrt_fusion), kind=kOutput, calls=%fused_computation.45 | convolution fusion | flops 269221888 | bytes 2884096 | tf_op jit(solution)/shard_map/dot_general | solution.py:87
  90.0 0.7 pad_maximum_fusion
  90.7 3.3 %all-to-all-start = ((bf16[128,4,128]{0,2,1:T(8,128)(2,1)}), bf16[128,4,128]{0,2,1:T(8,128)(2,1)S(1)}, u32[]{:S(2)}, u32[]{:S(2)}) async-start(bf16[128,4,128]{0,2,1:T(8,128)(2,1)} %bitcast.4), calls=%async_computation | async-start | bytes 262144 | tf_op jit(solution)/shard_map/all_to_all | solution.py:102
  94.0 0.1 fusion.35
  94.1 0.1 copy.36
  94.2 0.1 copy.35
  94.3 4.2 %all-to-all-done = bf16[128,4,128]{0,2,1:T(8,128)(2,1)S(1)} async-done(((bf16[128,4,128]{0,2,1:T(8,128)(2,1)}), bf16[128,4,128]{0,2,1:T(8,128)(2,1)S(1)}, u32[]{:S(2)}, u32[]{:S(2)}) %all-to-all-start) | async-done | bytes 131104 | tf_op jit(solution)/shard_map/all_to_all | solution.py:102
  98.6 0.1 copy.33
  98.7 0.1 reshape.178
  98.7 7.1 %while.11 = (s32[]{:T(128)}, bf16[2,256,2,64]{1,3,2,0:T(8,128)(2,1)S(1)}, s32[2]{0:T(128)S(1)}, s32[512]{0:T(512)S(1)}, bf16[512,2,64]{0,2,1:T(8,128)(2,1)S(1)},...) while((s32[]{:T(128)}, ...), condition=%wide.region_7.8_spmd.clone, body=%wide.region_4.7_spmd.clone.sunk | while | flops 103450368 | bytes 3943619 | solution.py:65
  98.8 0.6 dynamic_slice.31
  100.0 0.1 dynamic_slice.32
  100.1 0.2 fusion.56
  100.3 0.6 fusion.57
  100.9 0.3 fusion.58
  101.2 1.1 fusion.59
  102.3 0.6 dynamic_slice.31
  103.6 0.1 dynamic_slice.32
  103.7 0.2 fusion.56
  103.8 0.6 fusion.57
  104.4 0.3 fusion.58
  104.8 1.1 fusion.59
  105.9 0.1 copy.37
  106.0 0.1 all_to_all.44
  106.1 7.0 %all_to_all.51 = bf16[4,128,128]{1,2,0:T(8,128)(2,1)S(1)} all-to-all(bf16[4,128,128]{1,2,0:T(8,128)(2,1)S(1)} %copy.38), channel_id=1, replica_groups=mesh['dp'=8,'seq'=4] {'seq'}, dimensions={0} | all-to-all | bytes 262144 | tf_op jit(solution)/shard_map/all_to_all | solution.py:110
  113.1 0.8 copy.39
  (11 shorter events, 0.1 us)
Async XLA Ops:
  6.5 71.7 %copy-start = (bf16[128,2048]{1,0:T(8,128)(2,1)S(1)}, bf16[128,2048]{1,0:T(8,128)(2,1)}, u32[]{:S(2)}) copy-start(bf16[128,2048]{1,0:T(8,128)(2,1)} %param.7) | copy-start | bytes 1572868
  6.5 39.4 %copy-start.1 = (bf16[256,128]{1,0:T(8,128)(2,1)S(1)}, bf16[256,128]{1,0:T(8,128)(2,1)}, u32[]{:S(2)}) copy-start(bf16[256,128]{1,0:T(8,128)(2,1)} %param.10) | copy-start | bytes 196612
  6.5 80.8 %all-gather.2.cloned.1.call-start = ((), (), s32[]{:S(2)}) async-start(), calls=%async_computation.3 | async-start | bytes 2359296 | tf_op jit(solution)/shard_map/all_gather | solution.py:82
  79.3 7.9 %all-to-all-start.1 = ((bf16[128,4,128]{0,2,1:T(8,128)(2,1)}), bf16[128,4,128]{0,2,1:T(8,128)(2,1)S(1)}, u32[]{:S(2)}, u32[]{:S(2)}) async-start(bf16[128,4,128]{0,2,1:T(8,128)(2,1)} %bitcast.8), calls=%async_computation.1 | async-start | bytes 262144 | tf_op jit(solution)/shard_map/all_to_all | solution.py:103
  90.7 7.9 %all-to-all-start = ((bf16[128,4,128]{0,2,1:T(8,128)(2,1)}), bf16[128,4,128]{0,2,1:T(8,128)(2,1)S(1)}, u32[]{:S(2)}, u32[]{:S(2)}) async-start(bf16[128,4,128]{0,2,1:T(8,128)(2,1)} %bitcast.4), calls=%async_computation | async-start | bytes 262144 | tf_op jit(solution)/shard_map/all_to_all | solution.py:102
Sparse Core Ops, SparseCore 0:
  9.5 57.2 all-gather.1
where the time goes:
time: 121 us
  blocking collectives  73.4 us (61%)
  between operations  13.6 us (11%)
  waiting for transfers between devices  9.54 us (8%)
  matrix products  8.37 us (7%)
  starting transfers between devices  6.65 us (5%)
  other arithmetic  4.16 us (3%)
  local copies, waits for them, and re-layouts  3.63 us (3%)
  loops' own time  1.41 us (1%)
    all_gather x1, blocking collectives, shards(): lax.all_gather(key_weight, 'dp', axis=0, tiled=True)  34.1 us
    all_gather x1, blocking collectives, shards(): lax.all_gather(value_weight, 'dp', axis=0, tiled=True)  32.3 us
    all_to_all x1, blocking collectives, shards(): lax.all_to_all(mixed_heads, 'seq', split_axis=0, concat_axis=1, tiled=True)  6.99 us
    all_to_all x1, waiting for transfers between devices, shards(): lax.all_to_all(repeated, 'seq', split_axis=1, concat_axis=0, tiled=True)  4.56 us
    dot_general x3, matrix products, shards(): jnp.dot(normed, piece, preferred_element_type=jnp.float32)  4.36 us
    all_to_all x1, waiting for transfers between devices, shards(): lax.all_to_all(query_rot, 'seq', split_axis=1, concat_axis=0, tiled=True)  4.25 us
    all_to_all x1, starting transfers between devices, shards(): lax.all_to_all(repeated, 'seq', split_axis=1, concat_axis=0, tiled=True)  3.33 us
    all_to_all x1, starting transfers between devices, shards(): lax.all_to_all(query_rot, 'seq', split_axis=1, concat_axis=0, tiled=True)  3.33 us
  transfers between devices with their start and end apart: 3, of which 2 were waited for; matrix products, arithmetic and copies ran while one was open for 5% of the time, Pallas kernels for 0%

commit v1 on v0

--- a/solution.py
+++ b/solution.py
@@ -99,7 +99,12 @@
     key_value = jnp.concatenate([key_rot, value_cast], axis=2)
     repeated = jnp.repeat(key_value, seq_count // kv_heads, axis=1).reshape(tok_count, -1)
     query_heads, kv_local = (
-        lax.all_to_all(query_rot, "seq", split_axis=1, concat_axis=0, tiled=True),
+        jnp.concatenate(
+            lax.all_to_all(
+                jnp.stack(jnp.split(query_rot, lax.axis_size("seq"), axis=1)), "seq", 0, 0
+            ),
+            axis=0,
+        ),
         lax.all_to_all(repeated, "seq", split_axis=1, concat_axis=0, tiled=True),
     )
     key_local = kv_local[:, :head_dim]

time: 121 us -> 122 us (level)
  no operation moved by 1% of the time
where the time goes in v1:
time: 122 us; the launch traced here: 121 us
  blocking collectives  73.4 us (60%)
  between operations  13.6 us (11%)
  waiting for transfers between devices  9.53 us (8%)
  matrix products  8.37 us (7%)
  starting transfers between devices  6.65 us (5%)
  other arithmetic  4.19 us (3%)
  local copies, waits for them, and re-layouts  4.15 us (3%)
  loops' own time  1.41 us (1%)
    all_gather x1, blocking collectives, shards(): lax.all_gather(key_weight, 'dp', axis=0, tiled=True)  34.1 us
    all_gather x1, blocking collectives, shards(): lax.all_gather(value_weight, 'dp', axis=0, tiled=True)  32.3 us
    all_to_all x1, blocking collectives, shards(): lax.all_to_all(mixed_heads, 'seq', split_axis=0, concat_axis=1, tiled=True)  6.99 us
    all_to_all x1, waiting for transfers between devices, shards(): lax.all_to_all(repeated, 'seq', split_axis=1, concat_axis=0, tiled=True)  4.56 us
    dot_general x3, matrix products, shards(): jnp.dot(normed, piece, preferred_element_type=jnp.float32)  4.36 us
    all_to_all x1, waiting for transfers between devices, shards(): lax.all_to_all(jnp.stack(jnp.split(query_rot, lax.axis_size('seq'), axis=...  4.25 us
    all_to_all x1, starting transfers between devices, shards(): lax.all_to_all(repeated, 'seq', split_axis=1, concat_axis=0, tiled=True)  3.33 us
    all_to_all x1, starting transfers between devices, shards(): lax.all_to_all(jnp.stack(jnp.split(query_rot, lax.axis_size('seq'), axis=...  3.33 us
  transfers between devices with their start and end apart: 3, of which 2 were waited for; matrix products, arithmetic and copies ran while one was open for 5% of the time, Pallas kernels for 0%

profile of v1, /device:TPU:0, one launch (start us, length us, event | category | flops | bytes accessed | tf_op | source)
XLA Modules:
  0.0 121.3 jit_solution(9731737674602260007)
XLA Ops:
  6.5 0.0 all-gather.2.cloned.1.call-start
  6.5 0.7 all-gather.2.cloned.1.call-update
  7.3 0.8 reduce-window.8
  8.1 0.7 select_reduce_fusion
  8.9 0.1 dynamic-slice_convert_fusion
  8.9 1.2 %fusion.23 = f32[128]{0:T(128)S(1)} fusion(bf16[128,2048]{1,0:T(8,128)(2,1)} %param.7), kind=kLoop, calls=%fused_computation.27 | loop fusion | flops 786304 | bytes 524800 | tf_op jit(solution)/shard_map/reduce_sum | solution.py:15
  10.2 0.1 multiply_cosine_fusion
  10.3 34.1 %all_gather.10 = bf16[2048,128]{1,0:T(8,128)(2,1)S(1)} all-gather(bf16[256,128]{1,0:T(8,128)(2,1)} %param.9), channel_id=1, replica_groups=mesh['dp'=8,'seq'=4] {'dp'}, dimensions={0}, use_global_device_ids=true | all-gather | bytes 589824 | tf_op jit(solution)/shard_map/all_gather | solution.py:83
  44.5 1.4 %fusion.26 = f32[128,128]{0,1:T(8,128)S(1)} fusion(bf16[2048,128]{1,0:T(8,128)(2,1)S(1)} %all_gather.10, bf16[128,2048]{1,0:T(8,128)(2,1)} %param.7, f32[128]{0:T(128)S(1)} %add_rsqrt_fusion), kind=kOutput, calls=%fused_computation.45 | convolution fusion | flops 67895296 | bytes 1114624 | tf_op jit(solution)/shard_map/dot_general | solution.py:87
  45.9 0.0 copy-done.1
  45.9 32.3 %all_gather.11 = bf16[2048,128]{1,0:T(8,128)(2,1)S(1)} all-gather(bf16[256,128]{1,0:T(8,128)(2,1)S(1)} %copy-done.1), channel_id=1, replica_groups=mesh['dp'=8,'seq'=4] {'dp'}, dimensions={0}, use_global_device_ids=true | all-gather | bytes 589824 | tf_op jit(solution)/shard_map/all_gather | solution.py:84
  78.2 0.0 copy-done
  78.2 0.4 convolution_convert_fusion.1
  78.7 0.7 broadcast_in_dim.16
  79.3 3.3 %all-to-all-start.1 = ((bf16[128,4,128]{0,2,1:T(8,128)(2,1)}), bf16[128,4,128]{0,2,1:T(8,128)(2,1)S(1)}, u32[]{:S(2)}, u32[]{:S(2)}) async-start(bf16[128,4,128]{0,2,1:T(8,128)(2,1)} %bitcast.11), calls=%async_computation.1 | async-start | bytes 262144 | tf_op jit(solution)/shard_map/all_to_all | solution.py:108
  82.7 4.6 %all-to-all-done.1 = bf16[128,4,128]{0,2,1:T(8,128)(2,1)S(1)} async-done(((bf16[128,4,128]{0,2,1:T(8,128)(2,1)}), bf16[128,4,128]{0,2,1:T(8,128)(2,1)S(1)}, u32[]{:S(2)}, u32[]{:S(2)}) %all-to-all-start.1) | async-done | bytes 131104 | tf_op jit(solution)/shard_map/all_to_all | solution.py:108
  87.2 0.1 copy.58
  87.4 0.0 all-gather.2.cloned.1.call-done
  87.4 2.6 %fusion.28 = f32[128,512]{0,1:T(8,128)S(1)} fusion(bf16[2048,512]{1,0:T(8,128)(2,1)} %all-gather.2.cloned.1.call-done, bf16[128,2048]{1,0:T(8,128)(2,1)S(1)} %copy-done, f32[128]{0:T(128)S(1)} %add_rsqrt_fusion), kind=kOutput, calls=%fused_computation.46 | convolution fusion | flops 269221888 | bytes 2884096 | tf_op jit(solution)/shard_map/dot_general | solution.py:87
  90.0 0.1 copy.53
  90.2 0.1 copy.56
  90.3 0.1 copy.55
  90.4 0.1 copy.54
  90.5 0.7 pad_maximum_fusion.1
  91.2 3.3 %all-to-all-start = ((bf16[4,128,128]{2,1,0:T(8,128)(2,1)}), bf16[4,128,128]{2,1,0:T(8,128)(2,1)S(1)}, u32[]{:S(2)}, u32[]{:S(2)}) async-start(bf16[4,128,128]{2,1,0:T(8,128)(2,1)} %pad_maximum_fusion.1), calls=%async_computation | async-start | bytes 262144 | tf_op jit(solution)/shard_map/all_to_all | solution.py:103
  94.5 0.1 fusion.35
  94.7 0.1 copy.60
  94.8 0.1 copy.59
  94.9 4.2 %all-to-all-done = bf16[4,128,128]{2,1,0:T(8,128)(2,1)S(1)} async-done(((bf16[4,128,128]{2,1,0:T(8,128)(2,1)}), bf16[4,128,128]{2,1,0:T(8,128)(2,1)S(1)}, u32[]{:S(2)}, u32[]{:S(2)}) %all-to-all-start) | async-done | bytes 131104 | tf_op jit(solution)/shard_map/all_to_all | solution.py:103
  99.1 0.1 copy.57
  99.3 0.1 reshape_reshape.4
  99.3 7.1 %while.11 = (s32[]{:T(128)}, bf16[2,256,2,64]{1,3,2,0:T(8,128)(2,1)S(1)}, s32[2]{0:T(128)S(1)}, s32[512]{0:T(512)S(1)}, bf16[512,2,64]{0,2,1:T(8,128)(2,1)S(1)},...) while((s32[]{:T(128)}, ...), condition=%wide.region_7.8_spmd.clone, body=%wide.region_4.7_spmd.clone.sunk | while | flops 103450368 | bytes 3943619 | solution.py:65
  99.4 0.6 dynamic_slice.31
  100.6 0.1 dynamic_slice.32
  100.7 0.2 fusion.57
  100.9 0.6 fusion.58
  101.4 0.3 fusion.59
  101.8 1.1 fusion.60
  102.9 0.6 dynamic_slice.31
  104.2 0.1 dynamic_slice.32
  104.3 0.2 fusion.57
  104.4 0.6 fusion.58
  105.0 0.3 fusion.59
  105.4 1.1 fusion.60
  106.5 0.1 copy.61
  106.6 0.1 all_to_all.36
  106.7 7.0 %all_to_all.43 = bf16[4,128,128]{1,2,0:T(8,128)(2,1)S(1)} all-to-all(bf16[4,128,128]{1,2,0:T(8,128)(2,1)S(1)} %copy.62), channel_id=1, replica_groups=mesh['dp'=8,'seq'=4] {'seq'}, dimensions={0} | all-to-all | bytes 262144 | tf_op jit(solution)/shard_map/all_to_all | solution.py:115
  113.7 0.8 copy.63
  (15 shorter events, 0.1 us)
Async XLA Ops:
  6.5 71.7 %copy-start = (bf16[128,2048]{1,0:T(8,128)(2,1)S(1)}, bf16[128,2048]{1,0:T(8,128)(2,1)}, u32[]{:S(2)}) copy-start(bf16[128,2048]{1,0:T(8,128)(2,1)} %param.7) | copy-start | bytes 1572868
  6.5 39.4 %copy-start.1 = (bf16[256,128]{1,0:T(8,128)(2,1)S(1)}, bf16[256,128]{1,0:T(8,128)(2,1)}, u32[]{:S(2)}) copy-start(bf16[256,128]{1,0:T(8,128)(2,1)} %param.10) | copy-start | bytes 196612
  6.5 80.8 %all-gather.2.cloned.1.call-start = ((), (), s32[]{:S(2)}) async-start(), calls=%async_computation.3 | async-start | bytes 2359296 | tf_op jit(solution)/shard_map/all_gather | solution.py:82
  79.3 7.9 %all-to-all-start.1 = ((bf16[128,4,128]{0,2,1:T(8,128)(2,1)}), bf16[128,4,128]{0,2,1:T(8,128)(2,1)S(1)}, u32[]{:S(2)}, u32[]{:S(2)}) async-start(bf16[128,4,128]{0,2,1:T(8,128)(2,1)} %bitcast.11), calls=%async_computation.1 | async-start | bytes 262144 | tf_op jit(solution)/shard_map/all_to_all | solution.py:108
  91.2 7.9 %all-to-all-start = ((bf16[4,128,128]{2,1,0:T(8,128)(2,1)}), bf16[4,128,128]{2,1,0:T(8,128)(2,1)S(1)}, u32[]{:S(2)}, u32[]{:S(2)}) async-start(bf16[4,128,128]{2,1,0:T(8,128)(2,1)} %pad_maximum_fusion.1), calls=%async_computation | async-start | bytes 262144 | tf_op jit(solution)/shard_map/all_to_all | solution.py:103
Sparse Core Ops, SparseCore 0:
  9.5 57.2 all-gather.1
